TPU v7x, 256 devices: a whole 4x4x8 slice. The times are simulated.
256 devices in a mesh: req: 8 (over y, core), vocab: 32 (over x, z).
Axes of the slice: x: 4, y: 4, z: 8, core: 2. Of those that a mesh axis runs over, the one named last changes fastest.
Arguments:
- hidden_rows: bfloat16 [8192, 2048], P(('req', 'vocab')), may hold values from -20 to 20
- norm_gain: float32 [2048], replicated, may hold values from 0.1 to 1.9
- head_weight: bfloat16 [2048, 81920], P(None, 'vocab'), may hold values from -10 to 10
- token_ids: int32 [8192], P('req'), may hold values from 0 to 81919
- live_count: int32 [256], P(('req', 'vocab')), may hold values from 1 to 32, as said below
Outputs:
- logprob: float32 [8192], P(('req', 'vocab'))
- entropy: float32 [8192], P(('req', 'vocab'))
Inputs may be any that keep to these rules, and one draw needn't show every extreme that they name: `live_count`: the live rows of an owner are its first ones; some owner has all 32 live in every draw.
All inputs are finite; a program needn't handle non-finite values.
Results may differ from a plain program's by a relative error of at most 0.012.
Values may be sent and summed in bfloat16 or wider, within the bound.
A program may use at most 64 MiB of HBM per device.

v0:
```python
import jax
import jax.numpy as jnp
from jax import lax
from jax.sharding import PartitionSpec as P


def local_stats(row_block, labels, columns, first_col):
    logits = jnp.dot(row_block, columns, preferred_element_type=jnp.float32)
    row_top = jnp.max(logits, axis=1)
    shifted = logits - row_top[:, None]
    powers = jnp.exp(shifted)
    row_total = jnp.sum(powers, axis=1)
    row_spread = jnp.sum(powers * shifted, axis=1)
    width = columns.shape[1]
    offset = labels - first_col
    inside = (offset >= 0) & (offset < width)
    chosen = jnp.take_along_axis(logits, jnp.clip(offset, 0, width - 1)[:, None], axis=1)[:, 0]
    row_picked = jnp.where(inside, chosen, 0.0)
    return (row_top, row_total, row_spread, row_picked)


def rescale(row_top, row_total, row_spread, global_top):
    factor = jnp.exp(row_top - global_top)
    return (row_total * factor, (row_spread + (row_top - global_top) * row_total) * factor)


def finish(global_top, row_total, row_spread, row_picked, live_count, own_rows):
    log_total = jnp.log(row_total)
    logprob = row_picked - global_top - log_total
    entropy = log_total - row_spread / row_total
    live = jnp.arange(own_rows, dtype=jnp.int32) < live_count[0]
    return (jnp.where(live, logprob, 0.0), jnp.where(live, entropy, 0.0))


def own_slice(array, start, own_rows):
    return lax.dynamic_slice_in_dim(array, start, own_rows, 0)


def per_device(hidden_rows, norm_gain, head_weight, token_ids, live_count):
    own_rows = hidden_rows.shape[0]
    shard_width = head_weight.shape[1]
    values = hidden_rows.astype(jnp.float32)
    squares = jnp.mean(values * values, axis=1)
    normed = (values * lax.rsqrt(squares + 1e-06)[:, None] * norm_gain[None, :]).astype(
        jnp.bfloat16
    )
    gathered = lax.all_gather(normed, "vocab", axis=0, tiled=True)
    first_col = lax.axis_index("vocab") * shard_width
    row_top, row_total, row_spread, row_picked = local_stats(
        gathered, token_ids, head_weight, first_col
    )
    start = lax.axis_index("vocab") * own_rows
    global_top = lax.pmax(row_top, "vocab")
    scaled_total, scaled_spread = rescale(row_top, row_total, row_spread, global_top)
    summed_total, summed_spread, summed_picked = lax.psum(
        (scaled_total, scaled_spread, row_picked), "vocab"
    )
    return finish(
        own_slice(global_top, start, own_rows),
        own_slice(summed_total, start, own_rows),
        own_slice(summed_spread, start, own_rows),
        own_slice(summed_picked, start, own_rows),
        live_count,
        own_rows,
    )


def solution(mesh):
    placed = (P(("req", "vocab"), None), P(), P(None, "vocab"), P("req"), P(("req", "vocab")))
    return jax.shard_map(
        per_device,
        mesh=mesh,
        in_specs=placed,
        out_specs=(P(("req", "vocab")), P(("req", "vocab"))),
        check_vma=False,
    )
```

profile of v0, /device:TPU:16, one launch (start us, length us, event | category | flops | bytes accessed | tf_op | source)
XLA Modules:
  0.0 353.3 jit_solution(11047198373892118158)
XLA Ops:
  7.2 0.0 all-gather.2.cloned.1.call-start
  7.2 1.0 fusion.1
  8.3 1.7 fusion.3
  9.9 0.0 all-gather.2.cloned.1.call-update
  10.6 0.7 compare_select_fusion
  11.3 83.7 %all-gather.2.cloned.1.call-done = bf16[1024,2048]{1,0:T(8,128)(2,1)} async-done(((bf16[32,2048]{1,0:T(8,128)(2,1)}), bf16[1024,2048]{1,0:T(8,128)(2,1)}) %all-gather.2.cloned.1.call-update) | async-done | bytes 4194320 | tf_op jit(solution)/shard_map/all_gather | solution.py:47
  95.1 17.6 %fusion.7 = (f32[1024]{0:T(1024)S(1)}, f32[1024,2560]{1,0:T(8,128)}) fusion(bf16[1024,2048]{1,0:T(8,128)(2,1)} %all-gather.2.cloned.1.call-done, bf16[2048,2560]{1,0:T(8,128)(2,1)} %param.7), kind=kOutput, calls=%fused_computation.22 | convolution fusion | flops 10740038656 | bytes 25169920 | tf_op jit(solution)/shard_map/dot_general | solution.py:8
  112.7 0.0 copy-start
  112.7 71.8 %pmax.7 = f32[1024]{0:T(1024)S(1)} all-reduce(f32[1024]{0:T(1024)S(1)} %get-tuple-element.11), channel_id=1, replica_groups=mesh['req'=8,'vocab'=32] {'vocab'}, use_global_device_ids=true, to_apply=%region_3.0 | all-reduce | flops 1024 | bytes 8192 | tf_op jit(solution)/shard_map/pmax | solution.py:53
  184.5 6.3 %fusion = (f32[1024]{0:T(1024)S(1)}, f32[1024]{0:T(1024)S(1)}) fusion(f32[1024,2560]{1,0:T(8,128)} %get-tuple-element.12, f32[1024]{0:T(1024)S(1)} %get-tuple-element.11), kind=kLoop, calls=%fused_computation.3 | loop fusion | flops 10483712 | bytes 10498048 | tf_op jit(solution)/shard_map/reduce_sum | solution.py:13
  190.8 17.2 %gather_fusion = f32[1024]{0:T(1024)S(1)} fusion(f32[1024,2560]{1,0:T(8,128)} %get-tuple-element.12, s32[1024]{0:T(1024)S(1)} %bitcast.8), kind=kCustom, calls=%fused_computation | custom fusion | bytes 16384 | tf_op jit(solution)/shard_map/jit(take_along_axis)/gather | solution.py:17
  208.0 0.0 copy-done
  208.1 137.7 %all-reduce = (f32[1024]{0:T(1024)S(1)}, f32[1024]{0:T(1024)S(1)}, f32[1024]{0:T(1024)S(1)}) all-reduce(f32[1024]{0:T(1024)S(1)} %select_select_fusion, f32[1024]{0:T(1024)S(1)} %get-tuple-element.8, f32[1024]{0:T(1024)S(1)} %get-tuple-element.7), channel_id=1, replica_groups=mesh['req'=8,'vocab'=32] {'vocab'}, use_global_device_ids=true, to_apply=%region_1.0 | all-reduce | flops 3072 | bytes 24576 | tf_op jit(solution)/shard_map/psum | solution.py:55
  345.8 0.6 compare_select_fusion.1
  (6 shorter events, 0.1 us)
Async XLA Ops:
  7.2 87.9 %all-gather.2.cloned.1.call-start = ((), (), s32[]{:S(2)}) async-start(), calls=%async_computation | async-start | bytes 4325376 | tf_op jit(solution)/shard_map/all_gather | solution.py:47
  112.7 95.3 %copy-start = (s32[1024]{0:T(1024)S(1)}, s32[1024]{0:T(1024)}, u32[]{:S(2)}) copy-start(s32[1024]{0:T(1024)} %param.8) | copy-start | bytes 12292
Sparse Core Ops, SparseCore 0:
  10.6 84.4 all-gather.1
where the time goes:
time: 354 us; the launch traced here: 353 us
  blocking collectives  210 us (59%)
  waiting for transfers between devices  83.8 us (24%)
  matrix products  17.6 us (5%)
  local copies, waits for them, and re-layouts  17.2 us (5%)
  between operations  14.7 us (4%)
  other arithmetic  10.4 us (3%)
    psum x1, blocking collectives, per_device(): lax.psum((scaled_total, scaled_spread, row_picked), 'vocab')  138 us
    all_gather x1, waiting for transfers between devices, per_device(): gathered = lax.all_gather(normed, 'vocab', axis=0, tiled=True)  83.7 us
    pmax x1, blocking collectives, per_device(): global_top = lax.pmax(row_top, 'vocab')  71.8 us
    dot_general x1, matrix products, local_stats(): logits = jnp.dot(row_block, columns, preferred_element_type=jnp.float32)  17.6 us
    gather x1, local copies, waits for them, and re-layouts, local_stats(): jnp.take_along_axis(logits, jnp.clip(offset, 0, width - 1)[:, None], axis=1)  17.2 us
  transfers between devices with their start and end apart: 1, of which 1 were waited for; matrix products, arithmetic and copies ran while one was open for 0% of the time, Pallas kernels for 0%

commit v1 on v0

v1 whole, which is shorter than its diff:
```python
import functools

import jax
import jax.numpy as jnp
from jax import lax
from jax.experimental import pallas as pl
from jax.experimental.pallas import tpu as pltpu
from jax.sharding import PartitionSpec as P

X, Z = 4, 8
OWN = 32
HALF = 16
CHUNK = 128
PIECES = 2
GAP = 3
DIRECTIONS = ((1, 0), (-1, 0), (0, 1), (0, -1))
MESH = pl.DeviceIdType.MESH
LOWEST = -1e30

SLOTS = (
    (40, 56, 1, 39),
    (8, 24, 33, 7),
    (-1, -1, -1, -1),
    (47, 63, 2, 38),
    (9, 57, 34, 6),
    (41, 25, -1, 15),
    (10, 62, 3, 46),
    (42, 30, 35, 37),
    (55, 49, 58, 14),
    (18, 54, 11, 45),
    (50, 61, 43, 29),
    (22, 59, 36, 13),
    (53, 27, 19, 44),
    (51, 21, 12, 60),
    (23, 26, 4, 28),
    (52, 17, 20, 5),
    (48, 16, -1, 31),
)


def plan():
    arrival = {}
    transfers = {}
    for step, row in enumerate(SLOTS):
        for direction, code in enumerate(row):
            if code >= 0:
                transfers[code] = (step, direction)
                part, place = divmod(code, OWN)
                key = (part % 2, place)
                arrival[key] = max(arrival.get(key, -1), step)
    order = sorted(arrival, key=lambda key: (arrival[key], key))
    order += [(0, 0), (1, 0)]
    ready = [
        max(arrival.get(key, -1) for key in order[c : c + 8]) for c in range(0, len(order), 8)
    ]
    return transfers, order, ready


def kernel(hid, gain, tok, w_hbm, out, x, w, lg, ms, ss, ts, ps, tokt, msg, ret, w_sem, g_send, g_recv, r_send, r_recv):
    req = lax.axis_index("req")
    vocab = lax.axis_index("vocab")
    my_x, my_z = vocab // Z, vocab % Z
    width = w.shape[1]
    half = width // 2
    depth = x.shape[2]
    parts = PIECES // 2
    span = depth // parts
    transfers, order, ready = plan()
    place_of = {key: index for index, key in enumerate(order)}
    chunks = len(ready)

    def device(dx, dz):
        return (req, lax.rem(my_x + dx + X, X) * Z + lax.rem(my_z + dz + Z, Z))

    def piece_ref(code):
        part, place = divmod(code, OWN)
        chunk, index = divmod(place_of[(part % 2, place)], 8)
        return x.at[chunk, pl.ds(HALF * index, HALF), pl.ds(span * (part // 2), span)]

    weights = [
        pltpu.make_async_copy(
            w_hbm.at[:, pl.ds(half * h, half)], w.at[:, pl.ds(half * h, half)], w_sem.at[h]
        )
        for h in range(2)
    ]
    for copy in weights:
        copy.start()

    barrier = pltpu.get_barrier_semaphore()
    for dx, dz in DIRECTIONS:
        pl.semaphore_signal(barrier, inc=1, device_id=device(dx, dz), device_id_type=MESH)

    values = hid[...].astype(jnp.float32)
    squares = jnp.mean(values * values, axis=1, keepdims=True)
    normed = (values * lax.rsqrt(squares + 1e-06) * gain[...]).astype(jnp.bfloat16)
    for p in range(2):
        chunk, index = divmod(place_of[(p, 0)], 8)
        x[chunk, HALF * index : HALF * (index + 1), :] = normed[HALF * p : HALF * (p + 1), :]

    numbers = {code: n for n, code in enumerate(transfers)}
    gathers = {}
    for code, (step, direction) in transfers.items():
        part, place = divmod(code, OWN)
        dx, dz = DIRECTIONS[direction]
        source = part * OWN + (place // Z - dx) % X * Z + (place % Z - dz) % Z
        n = numbers[code]
        gathers[code] = pltpu.make_async_remote_copy(
            src_ref=piece_ref(source),
            dst_ref=piece_ref(code),
            send_sem=g_send.at[n],
            recv_sem=g_recv.at[n],
            device_id=device(dx, dz),
            device_id_type=MESH,
        )

    def send(step):
        if step < len(SLOTS):
            for code in SLOTS[step]:
                if code >= 0:
                    gathers[code].start()

    pl.semaphore_wait(barrier, len(DIRECTIONS))
    for step in range(GAP):
        send(step)

    first_col = vocab * width
    columns = (tok[...] - first_col).astype(jnp.float32)
    for g in range(tok.shape[0]):
        tokt[128 * g : 128 * (g + 1), :] = jnp.broadcast_to(columns[g : g + 1, :], (128, 128)).T

    lanes = lax.broadcasted_iota(jnp.int32, (CHUNK, 128), 1)
    lane_columns = lanes.astype(jnp.float32)
    rows = lax.broadcasted_iota(jnp.int32, (CHUNK, 128), 0)
    diagonal = lanes % HALF == rows % HALF
    segment = lanes // HALF

    def owner_of(key):
        return lax.rem(my_x - key[1] // Z + X, X) * Z + lax.rem(my_z - key[1] % Z + Z, Z)

    def dot(c, h):
        if c == 0:
            weights[h].wait()
        lg[h] = jnp.dot(
            x[c], w[:, half * h : half * (h + 1)], preferred_element_type=jnp.float32
        )

    def stats(c, h):
        keys = order[8 * c : 8 * c + 8]
        wanted = jnp.concatenate(
            [
                tokt[pl.ds(pl.multiple_of(owner_of(key) * OWN + HALF * key[0], HALF), HALF), :]
                for key in keys
            ],
            axis=0,
        )
        tiles = [lg[h, :, 128 * k : 128 * (k + 1)] for k in range(half // 128)]
        top = functools.reduce(jnp.maximum, tiles)
        if h == 0:
            total = spread = picked = jnp.zeros((CHUNK, 128), jnp.float32)
        else:
            before = ms[...]
            top = jnp.maximum(before, top)
            moved = before - top
            factor = jnp.exp(moved)
            total = ss[...]
            spread = (ts[...] + moved * total) * factor
            total = total * factor
            picked = ps[...]
        for k, tile in enumerate(tiles):
            shifted = tile - top
            power = jnp.exp(shifted)
            total = total + power
            spread = spread + power * shifted
            picked = jnp.where(wanted - (half * h + 128 * k) == lane_columns, tile, picked)
        if h == 0:
            ms[...], ss[...], ts[...], ps[...] = top, total, spread, picked
            return
        row_top = jnp.max(top, axis=1, keepdims=True)
        moved = top - row_top
        factor = jnp.exp(moved)
        row_spread = jnp.sum((spread + moved * total) * factor, axis=1, keepdims=True)
        row_total = jnp.sum(total * factor, axis=1, keepdims=True)
        row_picked = jnp.sum(picked, axis=1, keepdims=True)
        packed = jnp.where(
            segment >= 4,
            row_top,
            jnp.where(segment == 1, row_spread, jnp.where(segment == 2, row_picked, row_total)),
        )
        packed = jnp.where(diagonal, packed, 0.0)
        for i, key in enumerate(keys):
            line = jnp.sum(packed[HALF * i : HALF * (i + 1)], axis=0, keepdims=True)
            if key[1] == 0:
                ret[key[0] * OWN] = line
            else:
                msg[8 * c + i] = line
        for i, key in enumerate(keys):
            if key[1] != 0:
                returns[key].start()

    returns = {}
    for index, key in enumerate(order):
        if key[1] != 0:
            n = key[0] * OWN + key[1]
            returns[key] = pltpu.make_async_remote_copy(
                src_ref=msg.at[index],
                dst_ref=ret.at[n],
                send_sem=r_send.at[n],
                recv_sem=r_recv.at[n],
                device_id=device(-(key[1] // Z), -(key[1] % Z)),
                device_id_type=MESH,
            )

    steps = [(c, h) for c in range(chunks) for h in range(2)]
    done = 0

    def compute():
        nonlocal done
        dot(*steps[done])
        if done:
            stats(*steps[done - 1])
        done += 1

    for step, row in enumerate(SLOTS):
        for code in row:
            if code >= 0:
                gathers[code].wait_recv()
        send(step + GAP)
        if step % parts == parts - 1 and ready[steps[done][0]] <= step:
            compute()
    while done < len(steps):
        compute()
    stats(*steps[-1])

    for copy in gathers.values():
        copy.wait_send()
    for copy in returns.values():
        copy.wait_send()
    for copy in returns.values():
        copy.wait_recv()

    lane = lax.broadcasted_iota(jnp.int32, (1, 128), 1)
    seg = lane // HALF
    results = []
    for p in range(2):
        lines = [ret[p * OWN + i] for i in range(OWN)]
        tops = [pltpu.roll(line, 64, 1) for line in lines]
        top = functools.reduce(jnp.maximum, tops)
        sums = jnp.zeros((1, 128), jnp.float32)
        for line, shard_top in zip(lines, tops):
            moved = shard_top - top
            factor = jnp.where(seg == 2, 1.0, jnp.exp(moved))
            factor = jnp.where(seg == 3, factor * moved, factor)
            sums = sums + line * factor
        spread = pltpu.roll(sums, 112, 1) + pltpu.roll(sums, 80, 1)
        picked = pltpu.roll(sums, 96, 1)
        log_total = jnp.log(sums)
        results.append((picked - top - log_total, log_total - spread / sums))
    for i in range(2):
        second = pltpu.roll(results[1][i], HALF, 1)
        out[i : i + 1, :] = jnp.where(lane < HALF, results[0][i], second)


def per_device(hidden_rows, norm_gain, head_weight, token_ids, live_count):
    own, depth = hidden_rows.shape
    width = head_weight.shape[1]
    group = token_ids.shape[0]
    vmem = pl.BlockSpec(memory_space=pltpu.VMEM)
    stat = pltpu.VMEM((CHUNK, 128), jnp.float32)
    result = pl.pallas_call(
        kernel,
        out_shape=jax.ShapeDtypeStruct((2, 128), jnp.float32),
        in_specs=[vmem, vmem, vmem, pl.BlockSpec(memory_space=pl.ANY)],
        out_specs=vmem,
        scratch_shapes=[
            pltpu.VMEM((group // CHUNK, CHUNK, depth), jnp.bfloat16),
            pltpu.VMEM((depth, width), jnp.bfloat16),
            pltpu.VMEM((2, CHUNK, width // 2), jnp.float32),
            stat,
            stat,
            stat,
            stat,
            pltpu.VMEM((group, 128), jnp.float32),
            pltpu.VMEM((2 * OWN, 1, 128), jnp.float32),
            pltpu.VMEM((2 * OWN, 1, 128), jnp.float32),
            pltpu.SemaphoreType.DMA((2,)),
            pltpu.SemaphoreType.DMA((PIECES * (OWN - 1),)),
            pltpu.SemaphoreType.DMA((PIECES * (OWN - 1),)),
            pltpu.SemaphoreType.DMA((2 * OWN,)),
            pltpu.SemaphoreType.DMA((2 * OWN,)),
        ],
        compiler_params=pltpu.CompilerParams(
            collective_id=0, has_side_effects=True, vmem_limit_bytes=56 << 20
        ),
        name="head_stats",
    )(hidden_rows, norm_gain.reshape(1, depth), token_ids.reshape(group // 128, 128), head_weight)
    live = jnp.arange(own, dtype=jnp.int32) < live_count[0]
    return (
        jnp.where(live, result[0, :own], 0.0),
        jnp.where(live, result[1, :own], 0.0),
    )


def solution(mesh):
    placed = (P(("req", "vocab"), None), P(), P(None, "vocab"), P("req"), P(("req", "vocab")))
    return jax.shard_map(
        per_device,
        mesh=mesh,
        in_specs=placed,
        out_specs=(P(("req", "vocab")), P(("req", "vocab"))),
        check_vma=False,
    )
```

time: 354 us -> 49.4 us (0.14)
  blocking collectives: 210 us -> 0 us
  waiting for transfers between devices: 83.8 us -> 0 us
  Pallas kernels: 0 us -> 46.7 us
  matrix products: 17.6 us -> 0 us
  local copies, waits for them, and re-layouts: 17.2 us -> 0 us
  between operations: 14.7 us -> 1.29 us
  other arithmetic: 10.4 us -> 1.26 us
    psum x1 -> x0, blocking collectives: 138 us -> none  [per_device(): lax.psum((scaled_total, scaled_spread, row_picked), 'vocab')]
    all_gather x1 -> x0, waiting for transfers between devices: 83.7 us -> none  [per_device(): gathered = lax.all_gather(normed, 'vocab', axis=0, tiled=True)]
    pmax x1 -> x0, blocking collectives: 71.8 us -> none  [per_device(): global_top = lax.pmax(row_top, 'vocab')]
    pallas_call x0 -> x1, Pallas kernels: none -> 46.7 us  [per_device(): pl.pallas_call(kernel, out_shape=jax.ShapeDtypeStruct((2, 128), jnp.float...]
    dot_general x1 -> x0, matrix products: 17.6 us -> none  [local_stats(): logits = jnp.dot(row_block, columns, preferred_element_type=jnp.float32)]
    gather x1 -> x0, local copies, waits for them, and re-layouts: 17.2 us -> none  [local_stats(): jnp.take_along_axis(logits, jnp.clip(offset, 0, width - 1)[:, None], axis=1)]
    reduce_sum x2 -> x0, other arithmetic: 7.35 us -> none  [the longest x1 6.32 us: local_stats(): row_spread = jnp.sum(powers * shifted, axis=1)]
  transfers between devices with their start and end apart: 1 -> 0, of which waited for: 1 -> 0; matrix products, arithmetic and copies ran while one was open for 0% -> 0% of each run, Pallas kernels for 0% -> 0%
where the time goes in v1:
time: 49.4 us; the launch traced here: 49.2 us
  Pallas kernels  46.7 us (95%)
  between operations  1.29 us (3%)
  other arithmetic  1.26 us (3%)
    pallas_call x1, Pallas kernels, per_device(): pl.pallas_call(kernel, out_shape=jax.ShapeDtypeStruct((2, 128), jnp.float...  46.7 us
    select_n x1, other arithmetic, per_device(): jnp.where(live, result[1, :own], 0.0)  1.26 us

profile of v1, /device:TPU:16, one launch (start us, length us, event | category | flops | bytes accessed | tf_op | source)
XLA Modules:
  0.0 49.2 jit_solution(16469648362453555608)
XLA Ops:
  1.3 46.7 %head_stats.1 = f32[2,128]{1,0:T(2,128)} custom-call(bf16[32,2048]{1,0:T(8,128)(2,1)} %hid.1, f32[1,2048]{1,0:T(1,128)} %bitcast.8, s32[8,128]{1,0:T(8,128)} %bitcast.9, bf16[2048,2560]{1,0:T(8,128)(2,1)} %w_hbm.1), custom_call_target="tpu_custom_call" | custom-call | tf_op jit(solution)/shard_map/head_stats/pallas_call | solution.py:269
  48.0 1.3 %compare_select_fusion = (f32[32]{0:T(128)}, f32[32]{0:T(128)}) fusion(f32[2,128]{1,0:T(2,128)} %head_stats.1, s32[]{:T(128)} %bitcast.7), kind=kLoop, calls=%fused_computation | loop fusion | flops 96 | bytes 516 | tf_op jit(solution)/shard_map/jit(_where)/select_n | solution.py:299
